TPU v7x, 32 devices: a whole 2x2x4 slice. The times are simulated.
32 devices in a mesh: seq: 16 (over z, y, x), col: 2 (over core).
Axes of the slice: x: 2, y: 2, z: 4, core: 2. Of those that a mesh axis runs over, the one named last changes fastest.
Arguments:
- hidden: bfloat16 [4, 96, 2304], P(None, None, 'seq'), may hold values from -6 to 6
- key_cache: bfloat16 [1152, 128, 2048], P('seq', None, 'col'), may hold values from -300 to 300
- value_cache: bfloat16 [1152, 128, 2048], P('seq', None, 'col'), may hold values from -6 to 6
- page_table: int32 [96, 128], replicated, may hold values from 0 to 1151, as said below
- cache_len: int32 [96], replicated, may hold values from 1 to 16380, as said below
- order: int32 [96], replicated, may hold values from 0 to 95, each once
- route_ids: int32 [4, 96, 2], replicated, may hold values from 0 to 7, all different within a row; in each aligned block of 96 rows (0 to 95, 96 to 191, ..., all dimensions but the last counted through in order) at most 48 rows name the same one
- w_qkv: bfloat16 [2304, 3, 2048], P('seq', None, 'col'), may hold values from -0.125 to 0.125
- w_out: bfloat16 [2048, 2304], P('col', 'seq'), may hold values from -0.125 to 0.125
- w_router: bfloat16 [2304, 8], replicated, may hold values from -0.125 to 0.125
- w_gate_up: bfloat16 [8, 2304, 2, 5760], P('col', None, None, 'seq'), may hold values from -0.125 to 0.125
- w_down: bfloat16 [8, 5760, 2304], P('col', 'seq'), may hold values from -0.109375 to 0.109375
Outputs:
- layer_out: bfloat16 [4, 96, 2304], P(None, None, 'seq')
- new_keys: bfloat16 [4, 96, 2048], P(None, None, 'col')
- new_values: bfloat16 [4, 96, 2048], P(None, None, 'col')
Inputs may be any that keep to these rules, and one draw needn't show every extreme that they name: `cache_len`: one request's cache holds exactly 16380 tokens; 4 requests hold more than 640 tokens, the others at most 640. `page_table`: for request r the entries 0 to ceil((cache_len[r] + 4) / 128) - 1 name pages that no other such entry names; later entries are never read. `order`: each request sits in exactly one batch slot. `route_ids`: the two experts of a row differ; in each step no expert is named by more than 48 requests.
All inputs are finite; a program needn't handle non-finite values.
Results may differ from a plain program's by a relative error of at most 0.011.
Values may be sent and summed in bfloat16 or wider, within the bound.
A program may use at most 256 MiB of HBM per device.

v0:
```python
import jax
import jax.numpy as jnp
from jax import lax
from jax.sharding import PartitionSpec as P

HEAD_DIM = 64
EPSILON = 1e-05
LOWEST = -1e30


def rotate(row_data, positions, head_dim):
    head_count = row_data.shape[1] // head_dim
    half_dim = head_dim // 2
    frequency = jnp.exp(
        -jnp.log(10000.0) * 2.0 * jnp.arange(half_dim, dtype=jnp.float32) / head_dim
    )
    angles = positions.astype(jnp.float32)[:, None] * frequency[None, :]
    cosine = jnp.cos(angles)[:, None, :]
    sines = jnp.sin(angles)[:, None, :]
    by_head = row_data.reshape(row_data.shape[0], head_count, head_dim)
    front_half = by_head[:, :, :half_dim]
    back_half = by_head[:, :, half_dim:]
    turned = jnp.concatenate(
        [front_half * cosine - back_half * sines, back_half * cosine + front_half * sines], axis=2
    )
    return turned.reshape(row_data.shape)


def local(
    hidden,
    key_cache,
    value_cache,
    page_table,
    cache_len,
    order,
    route_ids,
    w_qkv,
    w_out,
    w_router,
    w_gate_up,
    w_down,
):
    step_count = hidden.shape[0]
    requests = hidden.shape[1]
    width_loc = hidden.shape[2]
    pages_loc = key_cache.shape[0]
    page_size = key_cache.shape[1]
    cols_loc = key_cache.shape[2]
    heads_loc = cols_loc // HEAD_DIM
    width_all = width_loc * lax.axis_size("seq")
    experts_loc = w_gate_up.shape[0]
    ff_loc = w_gate_up.shape[3]
    expert_count = w_router.shape[1]
    expert_base = lax.axis_index("col") * experts_loc
    seq_index = lax.axis_index("seq")
    score_scale = HEAD_DIM ** (-0.5)
    placing = (order[:, None] == jnp.arange(requests)[None, :]).astype(jnp.bfloat16)
    needed = (cache_len + step_count + page_size - 1) // page_size
    columns = jnp.arange(page_table.shape[1])
    in_use = columns[None, :] < needed[:, None]
    local_pages = page_table - seq_index * pages_loc
    page_hits = in_use[:, :, None] & (
        local_pages[:, :, None] == jnp.arange(pages_loc)[None, None, :]
    )
    owned_by = jnp.any(page_hits, axis=1)
    page_starts = jnp.sum(jnp.where(page_hits, columns[None, :, None] * page_size, 0), axis=(0, 1))
    page_len = jnp.sum(jnp.where(owned_by, cache_len[:, None], 0), axis=0)
    is_valid = page_starts[:, None] + jnp.arange(page_size)[None, :] < page_len[:, None]
    owner_pages = owned_by.T
    owner_float = owner_pages.astype(jnp.float32)
    owner_half = owner_pages.astype(jnp.bfloat16)
    keys_local = key_cache.reshape(pages_loc, page_size, heads_loc, HEAD_DIM)
    values_local = value_cache.reshape(pages_loc, page_size, heads_loc, HEAD_DIM)
    w_proj = w_qkv.reshape(width_loc, 3 * cols_loc)
    w_pair = w_gate_up.reshape(experts_loc, width_all, 2 * ff_loc)
    expert_ids = jnp.arange(expert_count)
    known_keys = jnp.zeros((step_count, requests, cols_loc), jnp.bfloat16)
    known_values = jnp.zeros((step_count, requests, cols_loc), jnp.bfloat16)
    attend_known_keys = known_keys
    attend_known_values = known_values
    row_count = step_count * requests
    inputs = jnp.einsum("nsc,sr->nrc", hidden, placing, preferred_element_type=jnp.float32).astype(
        jnp.bfloat16
    )
    wide_in = inputs.astype(jnp.float32)
    squares = jnp.sum(wide_in * wide_in, axis=2)
    partial_value = jnp.dot(
        inputs.reshape(row_count, width_loc), w_proj, preferred_element_type=jnp.float32
    )
    squares, partial_value = lax.psum((squares, partial_value), "seq")
    inv_one = lax.rsqrt(squares.reshape(row_count) / width_all + EPSILON)
    partial_value = partial_value * inv_one[:, None]
    positions = (cache_len[None, :] + 0 + jnp.arange(step_count)[:, None]).reshape(row_count)
    query = rotate(partial_value[:, :cols_loc], positions, HEAD_DIM).astype(jnp.bfloat16)
    fresh_key = rotate(partial_value[:, cols_loc : 2 * cols_loc], positions, HEAD_DIM).astype(
        jnp.bfloat16
    )
    fresh_value = partial_value[:, 2 * cols_loc :].astype(jnp.bfloat16)
    attend_known_keys = attend_known_keys.at[0 : 0 + step_count].set(
        fresh_key.reshape(step_count, requests, cols_loc)
    )
    attend_known_values = attend_known_values.at[0 : 0 + step_count].set(
        fresh_value.reshape(step_count, requests, cols_loc)
    )
    query_heads = query.reshape(step_count, requests, heads_loc, HEAD_DIM)
    page_query = jnp.einsum(
        "pr,nrhd->nphd", owner_half, query_heads, preferred_element_type=jnp.float32
    ).astype(jnp.bfloat16)
    scores = (
        jnp.einsum("pthd,nphd->npth", keys_local, page_query, preferred_element_type=jnp.float32)
        * score_scale
    )
    in_page = is_valid[None, :, :, None]
    scores = jnp.where(in_page, scores, LOWEST)
    page_peak = jnp.max(scores, axis=2)
    owner_mask = owner_pages[None, :, :, None]
    req_peak = jnp.max(jnp.where(owner_mask, page_peak[:, :, None, :], LOWEST), axis=1)
    back_peak = jnp.max(jnp.where(owner_mask, req_peak[:, None, :, :], LOWEST), axis=2)
    weights = jnp.where(in_page, jnp.exp(scores - back_peak[:, :, None, :]), 0.0)
    page_total = jnp.sum(weights, axis=2)
    page_sums = jnp.einsum(
        "npth,pthd->nphd",
        weights.astype(jnp.bfloat16),
        values_local,
        preferred_element_type=jnp.float32,
    )
    weight_sum = jnp.einsum("pr,nph->nrh", owner_float, page_total, precision=lax.Precision.HIGHEST)
    value_sum = jnp.einsum(
        "pr,nphd->nrhd", owner_float, page_sums, precision=lax.Precision.HIGHEST
    ).reshape(step_count, requests, cols_loc)
    top_score = lax.pmax(req_peak, "seq")
    rescale = jnp.exp(req_peak - top_score)
    scaled_values = (
        value_sum.reshape(step_count, requests, heads_loc, HEAD_DIM) * rescale[..., None]
    ).reshape(step_count, requests, cols_loc)
    weight_sum, value_sum = lax.psum((weight_sum * rescale, scaled_values), "seq")
    known_heads = attend_known_keys.reshape(step_count, requests, heads_loc, HEAD_DIM)
    fresh_scores = (
        jnp.einsum("nrhd,urhd->nruh", query_heads, known_heads, preferred_element_type=jnp.float32)
        * score_scale
    )
    visible = jnp.arange(step_count)[None, :] <= 0 + jnp.arange(step_count)[:, None]
    seen = visible[:, None, :, None]
    fresh_scores = jnp.where(seen, fresh_scores, LOWEST)
    best_score = jnp.maximum(top_score, jnp.max(fresh_scores, axis=2))
    fresh_weights = jnp.where(seen, jnp.exp(fresh_scores - best_score[:, :, None, :]), 0.0)
    cache_factor = jnp.exp(top_score - best_score)
    denominator = weight_sum * cache_factor + jnp.sum(fresh_weights, axis=2)
    fresh_sums = jnp.einsum(
        "nruh,urhd->nrhd",
        fresh_weights.astype(jnp.bfloat16),
        attend_known_values.reshape(step_count, requests, heads_loc, HEAD_DIM),
        preferred_element_type=jnp.float32,
    )
    numerator = (
        value_sum.reshape(step_count, requests, heads_loc, HEAD_DIM) * cache_factor[..., None]
        + fresh_sums
    )
    attended = (
        (numerator / denominator[..., None]).reshape(row_count, cols_loc).astype(jnp.bfloat16)
    )
    projected = lax.psum(jnp.dot(attended, w_out, preferred_element_type=jnp.float32), "col")
    residual = (wide_in.reshape(row_count, width_loc) + projected).astype(jnp.bfloat16)
    chosen = route_ids.reshape(row_count, 2)
    mid_steps = residual.reshape(step_count, requests, width_loc)
    shard_rows = lax.all_gather(mid_steps, "seq", axis=2, tiled=True)
    flat_rows = shard_rows.reshape(row_count, shard_rows.shape[2])
    pair_sum = jnp.einsum("rc,ecf->ref", flat_rows, w_pair, preferred_element_type=jnp.float32)
    wide_rows = flat_rows.astype(jnp.float32)
    square_sum = jnp.sum(wide_rows * wide_rows, axis=1)
    router_sum = jnp.dot(flat_rows, w_router, preferred_element_type=jnp.float32)
    pair_sum, square_sum, router_sum = (pair_sum, square_sum, router_sum)
    inv_two = lax.rsqrt(square_sum / width_all + EPSILON)
    logits = router_sum * inv_two[:, None]
    first_pick = chosen[:, 0:1] == expert_ids[None, :]
    second_pick = chosen[:, 1:2] == expert_ids[None, :]
    first_share = jax.nn.sigmoid(
        jnp.sum(jnp.where(first_pick, logits, 0.0), axis=1)
        - jnp.sum(jnp.where(second_pick, logits, 0.0), axis=1)
    )
    gate_rows = jnp.where(first_pick, first_share[:, None], 0.0) + jnp.where(
        second_pick, 1.0 - first_share[:, None], 0.0
    )
    gate_local = lax.dynamic_slice_in_dim(gate_rows, expert_base, experts_loc, 1)
    pair_sum = pair_sum * inv_two[:, None, None]
    active = (jax.nn.silu(pair_sum[..., :ff_loc]) * pair_sum[..., ff_loc:]).astype(jnp.bfloat16)
    outputs = jnp.einsum("ref,efd->red", active, w_down, preferred_element_type=jnp.float32)
    weighted = jnp.sum(outputs * gate_local[:, :, None], axis=1)
    spread = lax.psum_scatter(weighted, "seq", scatter_dimension=1, tiled=True)
    mixture = lax.psum(spread, "col")
    layer_rows = (
        (residual.astype(jnp.float32) + mixture)
        .astype(jnp.bfloat16)
        .reshape(step_count, requests, width_loc)
    )
    return (layer_rows, attend_known_keys, attend_known_values)


def solution(mesh):
    placed = (
        P(None, None, "seq"),
        P("seq", None, "col"),
        P("seq", None, "col"),
        P(),
        P(),
        P(),
        P(),
        P("seq", None, "col"),
        P("col", "seq"),
        P(),
        P("col", None, None, "seq"),
        P("col", "seq", None),
    )
    return jax.shard_map(
        local,
        mesh=mesh,
        in_specs=placed,
        out_specs=(P(None, None, "seq"), P(None, None, "col"), P(None, None, "col")),
        check_vma=False,
    )
```

profile of v0, /device:TPU:0, one launch (start us, length us, event | category | flops | bytes accessed | tf_op | source)
XLA Modules:
  0.0 747.3 jit_solution(15203284363969013890)
XLA Ops:
  7.2 1.2 fusion.25
  8.5 0.7 copy-done.7
  9.4 1.2 copy.147
  10.6 3.0 fusion.35
  14.5 1.7 fusion.2
  16.3 45.7 %psum.43 = f32[4,96]{1,0:T(4,128)S(1)} all-reduce(f32[4,96]{1,0:T(4,128)S(1)} %get-tuple-element.66), channel_id=1, replica_groups=mesh['seq'=16,'col'=2] {'seq'}, use_global_device_ids=true, to_apply=%region_5.6 | all-reduce | flops 384 | bytes 3072 | tf_op jit(solution)/shard_map/psum | solution.py:90
  62.1 24.6 %copy.109 = bf16[72,128,1024]{1,2,0:T(8,128)(2,1)} copy(bf16[72,128,1024]{2,1,0:T(8,128)(2,1)} %param.21) | data formatting | bytes 37748736 | tf_op args[1]
  86.7 24.7 %copy.114 = bf16[72,128,1024]{1,2,0:T(8,128)(2,1)} copy(bf16[72,128,1024]{2,1,0:T(8,128)(2,1)} %param.22) | data formatting | bytes 37748736 | tf_op args[2]
  111.5 1.1 select_reduce_fusion
  112.8 0.9 multiply_cosine_fusion
  113.7 83.1 %all-reduce.5.cloned.1.call-done = f32[384,3072]{1,0:T(8,128)} async-done(((f32[384,3072]{1,0:T(8,128)}), f32[384,3072]{1,0:T(8,128)}) %all-reduce.5.cloned.1.call-update) | async-done | bytes 4718608 | tf_op jit(solution)/shard_map/psum | solution.py:90
  196.7 2.8 broadcast_multiply_fusion
  199.5 1.6 fusion.34
  201.1 1.0 copy-done.1
  202.6 1.0 subtract_convert_fusion
  203.7 0.6 convert_element_type.82
  204.8 2.6 copy.119
  207.4 2.2 copy.110
  209.6 9.4 %bitcast_reduce_fusion = (f32[4,72,16]{0,2,1:T(8,128)S(1)}, f32[72,16,4,128]{3,2,1,0:T(4,128)S(1)}) fusion(pred[72,128]{1,0:T(8,128)(4,1)S(1)} %add_compare_fusion, bf16[4,72,16,64]{3,0,2,1:T(4,128)(2,1)} %copy.110, bf16[72,128,16,64]{1,3,2,0:T(8,128)(2,1)} %bitcast.105), kind=kOutput, calls=%fused_computation.8 | convolution fusion | flops 77262336 | bytes 21851136 | tf_op jit(solution)/shard_map/pthd,nphd->npth/dot_general | solution.py:110
  219.6 0.8 select_reduce_fusion.2
  220.4 75.9 %pmax.7 = f32[4,96,16]{1,2,0:T(8,128)} all-reduce(f32[4,96,16]{1,2,0:T(8,128)S(1)} %select_reduce_fusion.2), channel_id=1, replica_groups=mesh['seq'=16,'col'=2] {'seq'}, use_global_device_ids=true, to_apply=%region_9.10 | all-reduce | flops 6144 | bytes 49152 | tf_op jit(solution)/shard_map/pmax | solution.py:131
  296.3 1.4 select_reduce_fusion.1
  297.6 3.0 copy.117
  300.7 1.6 multiply_subtract_fusion
  302.4 1.6 convert_element_type.87
  304.0 4.3 copy.118
  308.3 5.3 fusion.36
  313.6 3.7 copy.120
  317.3 1.4 copy.113
  318.7 1.1 fusion.22
  320.5 14.0 %convolution_bitcast_fusion = f32[4,72,16,64]{3,0,2,1:T(4,128)S(1)} fusion(bf16[72,128,16,64]{1,3,2,0:T(8,128)(2,1)} %bitcast.106, f32[72,16,4,128]{3,2,1,0:T(4,128)S(1)} %get-tuple-element.81, f32[4,72,16]{0,2,1:T(8,128)S(1)} %copy.113, pred[72,128]{1,0:T(8,128)(4,1)} %copy-done.12), kind=kOutput, calls=%fused_computation.24 | convolution fusion | flops 78446592 | bytes 22440960 | tf_op jit(solution)/shard_map/npth,pthd->nphd/dot_general | solution.py:121
  334.4 4.2 bitcast_multiply_fusion.1
  338.7 1.6 slice.111
  340.3 1.9 reshape.362
  342.2 5.0 fusion.20
  347.2 1.9 copy.127
  349.1 1.6 fusion.23
  350.7 3.2 copy.125
  353.9 3.7 fusion.12
  357.6 3.1 copy.126
  360.7 0.9 fusion.16
  361.7 72.0 %psum.45 = f32[4,96,16]{1,2,0:T(8,128)S(1)} all-reduce(f32[4,96,16]{1,2,0:T(8,128)S(1)} %fusion.16), channel_id=1, replica_groups=mesh['seq'=16,'col'=2] {'seq'}, use_global_device_ids=true, to_apply=%region_13.14 | all-reduce | flops 6144 | bytes 49152 | tf_op jit(solution)/shard_map/psum | solution.py:136
  433.6 0.8 multiply_add_fusion.1
  434.4 26.6 %all-reduce.7.cloned.1.call-done = f32[4,96,16,64]{1,3,2,0:T(8,128)} async-done(((f32[4,96,16,64]{1,3,2,0:T(8,128)}), f32[4,96,16,64]{1,3,2,0:T(8,128)}) %all-reduce.7.cloned.1.call-update) | async-done | bytes 1572880 | tf_op jit(solution)/shard_map/psum | solution.py:136
  461.1 2.8 fusion.9
  463.9 0.9 copy.131
  464.8 0.7 convert_element_type.90
  465.5 1.0 fusion.37
  466.8 17.3 %all-reduce.9.cloned.1.call-done = f32[384,144]{0,1:T(8,128)} async-done(((f32[384,144]{0,1:T(8,128)}), f32[384,144]{0,1:T(8,128)}) %all-reduce.9.cloned.1.call-update) | async-done | bytes 221200 | tf_op jit(solution)/shard_map/psum | solution.py:162
  484.2 1.0 add_convert_fusion.2
  485.1 0.8 reshape.350
  486.2 64.8 %all-gather.2.cloned.1.call-done = bf16[4,96,2304]{1,0,2:T(4,128)(2,1)} async-done(((bf16[4,96,144]{1,0,2:T(4,128)(2,1)}), bf16[4,96,2304]{1,0,2:T(4,128)(2,1)}) %all-gather.2.cloned.1.call-update) | async-done | bytes 1769488 | tf_op jit(solution)/shard_map/all_gather | solution.py:166
  550.9 4.2 multiply_reduce_fusion
  555.3 3.8 copy.132
  559.1 2.1 select_reduce_fusion.4
  561.2 10.3 %broadcast_multiply_fusion.1 = f32[384,4,720]{0,2,1:T(8,128)S(1)} fusion(f32[384]{0:T(512)S(1)} %rsqrt.27, bf16[384,2304,1]{1,0,2:T(8,128)(2,1)} %bitcast.108, bf16[4,2304,720]{1,2,0:T(8,128)(2,1)} %bitcast.117), kind=kOutput, calls=%fused_computation.19 | convolution fusion | flops 5097185280 | bytes 19465728 | tf_op jit(solution)/shard_map/rc,ecf->ref/dot_general | solution.py:168
  571.5 9.8 %fusion = f32[384,2304]{1,0:T(8,128)} fusion(bf16[4,360,2304]{2,1,0:T(8,128)(2,1)} %param.31, f32[384,4]{0,1:T(4,128)S(1)} %select_add_fusion, f32[384,4,720]{0,2,1:T(8,128)S(1)} %broadcast_multiply_fusion.1), kind=kOutput, calls=%fused_computation.1 | convolution fusion | flops 2557550592 | bytes 14604288 | tf_op jit(solution)/shard_map/ref,efd->red/dot_general | solution.py:187
  581.2 5.2 copy.134
  586.5 132.4 %reduce-scatter.2.cloned.1.call-done = f32[384,144]{0,1:T(8,128)} async-done(((f32[384,2304]{0,1:T(8,128)}), f32[384,144]{0,1:T(8,128)}) %reduce-scatter.2.cloned.1.call-update) | async-done | bytes 221200 | tf_op jit(solution)/shard_map/reduce_scatter | solution.py:189
  718.9 0.6 convert_element_type.96
  719.5 1.4 copy.136
  720.9 17.5 %all-reduce.11.cloned.1.call-done = f32[384,144]{0,1:T(8,128)} async-done(((f32[384,144]{0,1:T(8,128)}), f32[384,144]{0,1:T(8,128)}) %all-reduce.11.cloned.1.call-update) | async-done | bytes 221200 | tf_op jit(solution)/shard_map/psum | solution.py:190
  738.4 1.0 add_convert_fusion.1
  739.5 0.7 copy.135
  (77 shorter events, 4.6 us)
Async XLA Ops:
  7.2 458.3 %copy-start = (bf16[1024,144]{0,1:T(8,128)(2,1)S(1)}, bf16[1024,144]{0,1:T(8,128)(2,1)}, u32[]{:S(2)}) copy-start(bf16[1024,144]{0,1:T(8,128)(2,1)} %param.28) | copy-start | bytes 884740
  7.2 189.5 %all-reduce.5.cloned.1.call-start = ((), (), s32[]{:S(2)}) async-start(), calls=%async_computation.1 | async-start | bytes 9437184 | tf_op jit(solution)/shard_map/psum | solution.py:90
  8.5 0.7 copy-start.7
  13.6 0.7 copy-start.16
  13.6 0.8 copy-start.13
  13.6 447.4 %all-reduce.7.cloned.1.call-start = ((), (), s32[]{:S(2)}) async-start(), calls=%async_computation.2 | async-start | bytes 4194304 | tf_op jit(solution)/shard_map/psum | solution.py:136
  112.8 96.9 %copy-start.12 = (pred[72,128]{1,0:T(8,128)(4,1)}, pred[72,128]{1,0:T(8,128)(4,1)S(1)}, u32[]{:S(2)}) copy-start(pred[72,128]{1,0:T(8,128)(4,1)S(1)} %add_compare_fusion) | copy-start | bytes 27652
  199.5 2.6 copy-start.1
  219.1 81.6 %copy-start.9 = (f32[384,32]{0,1:T(8,128)S(1)}, f32[384,32]{0,1:T(8,128)}, u32[]{:S(2)}) copy-start(f32[384,32]{0,1:T(8,128)} %get-tuple-element.79) | copy-start | bytes 147460
  302.4 11.2 %copy-start.3 = (bf16[384,16,64]{0,2,1:T(8,128)(2,1)}, bf16[384,16,64]{0,2,1:T(8,128)(2,1)S(1)}, u32[]{:S(2)}) copy-start(bf16[384,16,64]{0,2,1:T(8,128)(2,1)S(1)} %maximum_convert_fusion) | copy-start | bytes 2359300
  313.6 6.2 copy-start.10
  318.7 15.7 %copy-start.6 = (f32[4,72,16]{0,2,1:T(8,128)}, f32[4,72,16]{0,2,1:T(8,128)S(1)}, u32[]{:S(2)}) copy-start(f32[4,72,16]{0,2,1:T(8,128)S(1)} %copy.113) | copy-start | bytes 55300
  338.7 145.5 %all-reduce.9.cloned.1.call-start = ((), (), s32[]{:S(2)}) async-start(), calls=%async_computation.3 | async-start | bytes 442368 | tf_op jit(solution)/shard_map/psum | solution.py:162
  340.3 6.9 copy-start.5
  342.2 6.9 copy-start.11
  463.9 2.7 copy-start.8
  464.8 21.2 %copy-start.15 = (s32[4,96,2]{1,2,0:T(2,128)S(1)}, s32[4,96,2]{1,2,0:T(2,128)}, u32[]{:S(2)}) copy-start(s32[4,96,2]{1,2,0:T(2,128)} %param.26) | copy-start | bytes 9220
  466.6 84.4 %all-gather.2.cloned.1.call-start = ((), (), s32[]{:S(2)}) async-start(), calls=%async_computation.4 | async-start | bytes 2506752 | tf_op jit(solution)/shard_map/all_gather | solution.py:166
  486.0 232.9 %reduce-scatter.2.cloned.1.call-start = ((), (), s32[]{:S(2)}) async-start(), calls=%async_computation.5 | async-start | bytes 3760128 | tf_op jit(solution)/shard_map/reduce_scatter | solution.py:189
  550.9 4.3 copy-start.2
  555.2 3.9 copy-start.14
  586.4 132.5 %copy-start.4 = (bf16[384,16,64]{0,2,1:T(8,128)(2,1)S(1)}, bf16[384,16,64]{0,2,1:T(8,128)(2,1)}, u32[]{:S(2)}) copy-start(bf16[384,16,64]{0,2,1:T(8,128)(2,1)} %copy-done.3) | copy-start | bytes 2359300
  586.4 152.0 %all-reduce.11.cloned.1.call-start = ((), (), s32[]{:S(2)}) async-start(), calls=%async_computation.6 | async-start | bytes 442368 | tf_op jit(solution)/shard_map/psum | solution.py:190
Sparse Core Ops, SparseCore 0:
  13.8 182.8 all-reduce.4
  338.8 122.2 all-reduce.6
  466.7 17.4 all-reduce.8
  487.4 63.4 all-gather.1
  586.5 132.2 reduce-scatter.1
  721.0 17.3 all-reduce.10
where the time goes:
time: 757 us; the launch traced here: 747 us
  waiting for transfers between devices  342 us (45%)
  blocking collectives  194 us (26%)
  local copies, waits for them, and re-layouts  102 us (13%)
  matrix products  65.3 us (9%)
  other arithmetic  29.9 us (4%)
  between operations  14.8 us (2%)
    reduce_scatter x1, waiting for transfers between devices, local(): spread = lax.psum_scatter(weighted, 'seq', scatter_dimension=1, tiled=True)  132 us
    psum x1, waiting for transfers between devices, local(): squares, partial_value = lax.psum((squares, partial_value), 'seq')  83.1 us
    pmax x1, blocking collectives, local(): top_score = lax.pmax(req_peak, 'seq')  75.9 us
    psum x1, blocking collectives, local(): lax.psum((weight_sum * rescale, scaled_values), 'seq')  72 us
    all_gather x1, waiting for transfers between devices, local(): shard_rows = lax.all_gather(mid_steps, 'seq', axis=2, tiled=True)  64.8 us
    unnamed x39, local copies, waits for them, and re-layouts  53.7 us
    psum x1, blocking collectives, local(): squares, partial_value = lax.psum((squares, partial_value), 'seq')  45.7 us
    psum x1, waiting for transfers between devices, local(): lax.psum((weight_sum * rescale, scaled_values), 'seq')  26.6 us
  transfers between devices with their start and end apart: 6, of which 6 were waited for; matrix products, arithmetic and copies ran while one was open for 11% of the time, Pallas kernels for 0%

commit v1 on v0

--- a/solution.py
+++ b/solution.py
@@ -159,7 +159,9 @@
     attended = (
         (numerator / denominator[..., None]).reshape(row_count, cols_loc).astype(jnp.bfloat16)
     )
-    projected = lax.psum(jnp.dot(attended, w_out, preferred_element_type=jnp.float32), "col")
+    projected = jnp.sum(
+        lax.all_gather(jnp.dot(attended, w_out, preferred_element_type=jnp.float32), "col"), axis=0
+    )
     residual = (wide_in.reshape(row_count, width_loc) + projected).astype(jnp.bfloat16)
     chosen = route_ids.reshape(row_count, 2)
     mid_steps = residual.reshape(step_count, requests, width_loc)

time: 757 us -> 735 us (0.971)
  waiting for transfers between devices: 342 us -> 321 us
    unnamed x6, waiting for transfers between devices: 0.1 us -> 133 us
    reduce_scatter x1 -> x0, waiting for transfers between devices: 132 us -> none  [local(): spread = lax.psum_scatter(weighted, 'seq', scatter_dimension=1, tiled=True)]
    psum x1 -> x0, waiting for transfers between devices: 17.3 us -> none  [local(): lax.psum(jnp.dot(attended, w_out, preferred_element_type=jnp.float32), 'c...]
    unnamed x39 -> x40, local copies, waits for them, and re-layouts: 53.7 us -> 58.8 us
  transfers between devices with their start and end apart: 6 -> 5, of which waited for: 6 -> 5; matrix products, arithmetic and copies ran while one was open for 11% -> 11% of each run, Pallas kernels for 0% -> 0%
where the time goes in v1:
time: 735 us; the launch traced here: 725 us
  waiting for transfers between devices  321 us (44%)
  blocking collectives  196 us (27%)
  local copies, waits for them, and re-layouts  99.9 us (14%)
  matrix products  64.6 us (9%)
  other arithmetic  28.4 us (4%)
  between operations  14.5 us (2%)
    unnamed x6, waiting for transfers between devices  133 us
    psum x1, waiting for transfers between devices, local(): squares, partial_value = lax.psum((squares, partial_value), 'seq')  83.1 us
    pmax x1, blocking collectives, local(): top_score = lax.pmax(req_peak, 'seq')  75.9 us
    psum x1, blocking collectives, local(): lax.psum((weight_sum * rescale, scaled_values), 'seq')  72 us
    all_gather x1, waiting for transfers between devices, local(): shard_rows = lax.all_gather(mid_steps, 'seq', axis=2, tiled=True)  61.5 us
    unnamed x40, local copies, waits for them, and re-layouts  58.8 us
    psum x1, blocking collectives, local(): squares, partial_value = lax.psum((squares, partial_value), 'seq')  45.7 us
    psum x1, waiting for transfers between devices, local(): lax.psum((weight_sum * rescale, scaled_values), 'seq')  26.5 us
  transfers between devices with their start and end apart: 5, of which 5 were waited for; matrix products, arithmetic and copies ran while one was open for 11% of the time, Pallas kernels for 0%

profile of v1, /device:TPU:0, one launch (start us, length us, event | category | flops | bytes accessed | tf_op | source)
XLA Modules:
  0.0 724.8 jit_solution(3737002149559758724)
XLA Ops:
  7.2 1.2 fusion.26
  8.5 0.6 copy-done.6
  9.4 1.2 copy.182
  10.6 3.0 fusion.36
  13.7 0.6 copy-done.16
  14.5 1.7 fusion.2
  16.3 45.7 %psum.36 = f32[4,96]{1,0:T(4,128)S(1)} all-reduce(f32[4,96]{1,0:T(4,128)S(1)} %get-tuple-element.66), channel_id=1, replica_groups=mesh['seq'=16,'col'=2] {'seq'}, use_global_device_ids=true, to_apply=%region_5.6 | all-reduce | flops 384 | bytes 3072 | tf_op jit(solution)/shard_map/psum | solution.py:90
  62.1 24.6 %copy.141 = bf16[72,128,1024]{1,2,0:T(8,128)(2,1)} copy(bf16[72,128,1024]{2,1,0:T(8,128)(2,1)} %param.21) | data formatting | bytes 37748736 | tf_op args[1]
  86.7 24.7 %copy.146 = bf16[72,128,1024]{1,2,0:T(8,128)(2,1)} copy(bf16[72,128,1024]{2,1,0:T(8,128)(2,1)} %param.22) | data formatting | bytes 37748736 | tf_op args[2]
  111.5 1.1 select_reduce_fusion
  112.8 0.9 multiply_cosine_fusion
  113.7 83.1 %all-reduce.4.cloned.1.call-done = f32[384,3072]{1,0:T(8,128)} async-done(((f32[384,3072]{1,0:T(8,128)}), f32[384,3072]{1,0:T(8,128)}) %all-reduce.4.cloned.1.call-update) | async-done | bytes 4718608 | tf_op jit(solution)/shard_map/psum | solution.py:90
  196.7 2.8 broadcast_multiply_fusion
  199.5 1.6 fusion.35
  201.1 1.0 copy-done.1
  202.6 1.0 subtract_convert_fusion
  203.7 0.6 convert_element_type.85
  204.8 2.6 copy.151
  207.4 2.2 copy.142
  209.7 9.4 %bitcast_reduce_fusion = (f32[4,72,16]{0,2,1:T(8,128)S(1)}, f32[72,16,4,128]{3,2,1,0:T(4,128)S(1)}) fusion(pred[72,128]{1,0:T(8,128)(4,1)S(1)} %add_compare_fusion, bf16[4,72,16,64]{3,0,2,1:T(4,128)(2,1)} %copy.142, bf16[72,128,16,64]{1,3,2,0:T(8,128)(2,1)} %bitcast.109), kind=kOutput, calls=%fused_computation.8 | convolution fusion | flops 77262336 | bytes 21851136 | tf_op jit(solution)/shard_map/pthd,nphd->npth/dot_general | solution.py:110
  219.6 0.8 select_reduce_fusion.2
  220.4 75.9 %pmax.7 = f32[4,96,16]{1,2,0:T(8,128)} all-reduce(f32[4,96,16]{1,2,0:T(8,128)S(1)} %select_reduce_fusion.2), channel_id=1, replica_groups=mesh['seq'=16,'col'=2] {'seq'}, use_global_device_ids=true, to_apply=%region_9.10 | all-reduce | flops 6144 | bytes 49152 | tf_op jit(solution)/shard_map/pmax | solution.py:131
  296.3 1.4 select_reduce_fusion.1
  297.7 3.0 copy.149
  300.7 1.6 multiply_subtract_fusion
  302.4 1.6 convert_element_type.90
  304.0 4.3 copy.150
  308.3 5.3 fusion.37
  313.6 3.7 copy.152
  317.3 1.4 copy.145
  318.7 1.1 fusion.23
  319.9 0.6 subtract_exponential_fusion.1
  320.5 14.0 %convolution_bitcast_fusion = f32[4,72,16,64]{3,0,2,1:T(4,128)S(1)} fusion(bf16[72,128,16,64]{1,3,2,0:T(8,128)(2,1)} %bitcast.110, f32[72,16,4,128]{3,2,1,0:T(4,128)S(1)} %get-tuple-element.81, f32[4,72,16]{0,2,1:T(8,128)S(1)} %copy.145, pred[72,128]{1,0:T(8,128)(4,1)} %copy-done.12), kind=kOutput, calls=%fused_computation.24 | convolution fusion | flops 78446592 | bytes 22440960 | tf_op jit(solution)/shard_map/npth,pthd->nphd/dot_general | solution.py:121
  334.5 4.2 bitcast_multiply_fusion.1
  338.8 1.6 slice.111
  340.3 1.9 reshape.361
  342.3 5.0 fusion.20
  347.2 1.9 copy.159
  349.2 1.6 fusion.24
  350.8 3.2 copy.157
  354.0 3.7 fusion.12
  357.6 3.1 copy.158
  360.8 0.9 fusion.16
  361.7 72.0 %psum.38 = f32[4,96,16]{1,2,0:T(8,128)S(1)} all-reduce(f32[4,96,16]{1,2,0:T(8,128)S(1)} %fusion.16), channel_id=1, replica_groups=mesh['seq'=16,'col'=2] {'seq'}, use_global_device_ids=true, to_apply=%region_13.14 | all-reduce | flops 6144 | bytes 49152 | tf_op jit(solution)/shard_map/psum | solution.py:136
  433.8 0.8 multiply_add_fusion.1
  434.5 26.5 %all-reduce.6.cloned.1.call-done = f32[4,96,16,64]{1,3,2,0:T(8,128)} async-done(((f32[4,96,16,64]{1,3,2,0:T(8,128)}), f32[4,96,16,64]{1,3,2,0:T(8,128)}) %all-reduce.6.cloned.1.call-update) | async-done | bytes 1572880 | tf_op jit(solution)/shard_map/psum | solution.py:136
  461.1 2.8 fusion.9
  463.9 0.9 copy.163
  464.8 0.7 convert_element_type.93
  465.8 2.1 all-gather
  468.9 0.7 fusion.22
  470.1 61.5 %all-gather.3.cloned.1.call-done = bf16[4,96,2304]{1,2,0:T(8,128)(2,1)} async-done(((bf16[4,96,144]{1,2,0:T(8,128)(2,1)}), bf16[4,96,2304]{1,2,0:T(8,128)(2,1)}) %all-gather.3.cloned.1.call-update) | async-done | bytes 1769488 | tf_op jit(solution)/shard_map/all_gather | solution.py:168
  531.5 2.4 multiply_reduce_fusion
  534.1 2.4 copy.165
  536.5 2.1 select_reduce_fusion.4
  538.6 10.3 %broadcast_multiply_fusion.1 = f32[384,4,720]{0,2,1:T(8,128)S(1)} fusion(f32[384]{0:T(512)S(1)} %rsqrt.27, bf16[384,2304,1]{1,0,2:T(8,128)(2,1)} %bitcast.113, bf16[4,2304,720]{1,2,0:T(8,128)(2,1)} %bitcast.123), kind=kOutput, calls=%fused_computation.19 | convolution fusion | flops 5097185280 | bytes 19465728 | tf_op jit(solution)/shard_map/rc,ecf->ref/dot_general | solution.py:170
  548.9 9.8 %fusion = f32[384,2304]{1,0:T(8,128)} fusion(bf16[4,360,2304]{2,1,0:T(8,128)(2,1)} %param.31, f32[384,4]{0,1:T(4,128)S(1)} %select_add_fusion, f32[384,4,720]{0,2,1:T(8,128)S(1)} %broadcast_multiply_fusion.1), kind=kOutput, calls=%fused_computation.1 | convolution fusion | flops 2557550592 | bytes 14604288 | tf_op jit(solution)/shard_map/ref,efd->red/dot_general | solution.py:189
  558.7 5.2 copy.178
  563.9 132.8 %reduce-scatter.4.cloned.1.call-done = f32[144,384]{1,0:T(8,128)} async-done(((f32[2304,384]{1,0:T(8,128)}), f32[144,384]{1,0:T(8,128)}) %reduce-scatter.4.cloned.1.call-update) | async-done | bytes 221200
  696.9 0.6 convert_element_type.100
  697.6 1.4 copy.169
  698.9 17.3 %all-reduce.8.cloned.1.call-done = f32[384,144]{0,1:T(8,128)} async-done(((f32[384,144]{0,1:T(8,128)}), f32[384,144]{0,1:T(8,128)}) %all-reduce.8.cloned.1.call-update) | async-done | bytes 221200 | tf_op jit(solution)/shard_map/psum | solution.py:192
  716.2 1.0 add_convert_fusion.1
  717.3 0.7 copy.168
  (77 shorter events, 4.9 us)
Async XLA Ops:
  7.2 458.3 %copy-start = (bf16[1024,144]{0,1:T(8,128)(2,1)S(1)}, bf16[1024,144]{0,1:T(8,128)(2,1)}, u32[]{:S(2)}) copy-start(bf16[1024,144]{0,1:T(8,128)(2,1)} %param.28) | copy-start | bytes 884740
  7.2 189.5 %all-reduce.4.cloned.1.call-start = ((), (), s32[]{:S(2)}) async-start(), calls=%async_computation.1 | async-start | bytes 9437184 | tf_op jit(solution)/shard_map/psum | solution.py:90
  8.5 0.7 copy-start.6
  13.6 0.7 copy-start.16
  13.6 0.8 copy-start.13
  13.6 447.4 %all-reduce.6.cloned.1.call-start = ((), (), s32[]{:S(2)}) async-start(), calls=%async_computation.2 | async-start | bytes 4194304 | tf_op jit(solution)/shard_map/psum | solution.py:136
  112.8 96.9 %copy-start.12 = (pred[72,128]{1,0:T(8,128)(4,1)}, pred[72,128]{1,0:T(8,128)(4,1)S(1)}, u32[]{:S(2)}) copy-start(pred[72,128]{1,0:T(8,128)(4,1)S(1)} %add_compare_fusion) | copy-start | bytes 27652
  199.5 2.6 copy-start.1
  219.1 81.6 %copy-start.9 = (f32[384,32]{0,1:T(8,128)S(1)}, f32[384,32]{0,1:T(8,128)}, u32[]{:S(2)}) copy-start(f32[384,32]{0,1:T(8,128)} %get-tuple-element.79) | copy-start | bytes 147460
  302.4 11.2 %copy-start.3 = (bf16[384,16,64]{0,2,1:T(8,128)(2,1)}, bf16[384,16,64]{0,2,1:T(8,128)(2,1)S(1)}, u32[]{:S(2)}) copy-start(bf16[384,16,64]{0,2,1:T(8,128)(2,1)S(1)} %maximum_convert_fusion) | copy-start | bytes 2359300
  313.6 6.2 copy-start.10
  318.7 15.7 %copy-start.8 = (f32[4,72,16]{0,2,1:T(8,128)}, f32[4,72,16]{0,2,1:T(8,128)S(1)}, u32[]{:S(2)}) copy-start(f32[4,72,16]{0,2,1:T(8,128)S(1)} %copy.145) | copy-start | bytes 55300
  338.7 192.8 %all-gather.3.cloned.1.call-start = ((), (), s32[]{:S(2)}) async-start(), calls=%async_computation.3 | async-start | bytes 2506752 | tf_op jit(solution)/shard_map/all_gather | solution.py:168
  340.3 6.9 copy-start.5
  342.3 6.9 copy-start.11
  465.5 3.5 copy-start.7
  465.5 4.4 copy-start.15
  469.7 227.0 %reduce-scatter.4.cloned.1.call-start = ((), (), s32[]{:S(2)}) async-start(), calls=%async_computation.5 | async-start | bytes 3760128
  531.5 2.5 copy-start.2
  534.0 2.5 copy-start.14
  563.8 133.1 %copy-start.4 = (bf16[384,16,64]{0,2,1:T(8,128)(2,1)S(1)}, bf16[384,16,64]{0,2,1:T(8,128)(2,1)}, u32[]{:S(2)}) copy-start(bf16[384,16,64]{0,2,1:T(8,128)(2,1)} %copy-done.3) | copy-start | bytes 2359300
  563.8 152.4 %all-reduce.8.cloned.1.call-start = ((), (), s32[]{:S(2)}) async-start(), calls=%async_computation.4 | async-start | bytes 442368 | tf_op jit(solution)/shard_map/psum | solution.py:192
Sparse Core Ops, SparseCore 0:
  13.8 182.9 all-reduce.3
  338.8 122.1 all-reduce.5
  469.8 61.7 all-gather.2
  564.0 132.6 reduce-scatter.3
  698.9 17.3 all-reduce.7
